TPU v7x, 32 devices: a whole 2x2x4 slice. The times are simulated.
32 devices in a mesh: clips: 2 (over y), tm: 4 (over z), rows: 2 (over x), chan: 2 (over core).
Axes of the slice: x: 2, y: 2, z: 4, core: 2. Of those that a mesh axis runs over, the one named last changes fastest.
Arguments:
- frames: bfloat16 [8, 8, 106, 384], P(('clips', 'tm'), 'rows', None, 'chan'), parts along dimension 0, may hold values from -18 to 18
- gain_attn: float32 [384], replicated, may hold values from 0.1 to 1.9
- w_qkv: bfloat16 [384, 1152], P('chan'), may hold values from -2.14330352 to 2.14330352
- w_out: bfloat16 [384, 384], replicated, may hold values from -3 to 3
- gain_conv: float32 [384], replicated, may hold values from 0.1 to 1.9
- w_conv: bfloat16 [3, 3, 3, 384, 384], P(None, None, None, None, 'chan'), may hold values from -0.0625 to 0.0625
Outputs:
- out: bfloat16 [8, 8, 106, 384], P(('clips', 'tm'), 'rows', None, 'chan'), parts along dimension 0
There are 2 independent parts, one for each index of `clips`. A program takes and returns all parts, laid end to end along the dimension named above; an argument that names none is the same for every part. Nothing has to cross between parts.
All inputs are finite; a program needn't handle non-finite values.
Results may differ from a plain program's by a relative error of at most 0.024.
Values may be sent and summed in bfloat16 or wider, within the bound.
A program may use at most 64 MiB of HBM per device.

v0:
```python
import jax
import jax.numpy as jnp
from jax import lax
from jax.sharding import PartitionSpec as P

epsilon = 1e-06


def extended_2(block, sides, width):
    for axis, dim in sides:
        count = lax.axis_size(axis)
        forward = [(i, i + 1) for i in range(count - 1)]
        backward = [(target, source) for source, target in forward]
        low = lax.ppermute(
            lax.slice_in_dim(block, block.shape[dim] - width, None, axis=dim), axis, forward
        )
        high = lax.ppermute(lax.slice_in_dim(block, 0, width, axis=dim), axis, backward)
        block = jnp.concatenate([low, block, high], axis=dim)
    return block


def shifted(array, axis, by):
    length = lax.axis_size(axis)
    pairs = [(i, i + by) for i in range(length) if 0 <= i + by < length]
    return lax.ppermute(array, axis, pairs)


def inv_rms(values):
    return lax.rsqrt(jnp.mean(values * values, axis=-1, keepdims=True) + epsilon)


def online_fold(queries, channels, score_scale, fold_carry, piece_rows):
    running, totals, weighted = fold_carry
    keys_piece = piece_rows[:, :channels]
    values_piece = piece_rows[:, channels:]
    scores = (
        jnp.einsum("qc,kc->qk", queries, keys_piece, preferred_element_type=jnp.float32)
        * score_scale
    )
    updated = jnp.max(scores, axis=1)
    factor = jnp.exp(running - updated)
    weights = jnp.exp(scores - updated[:, None])
    weighted = weighted * factor[:, None] + jnp.dot(
        weights.astype(jnp.bfloat16), values_piece, preferred_element_type=jnp.float32
    )
    return (updated, totals * factor + jnp.sum(weights, axis=1), weighted)


def empty_state(count, channels):
    return (
        jnp.full((count,), -jnp.inf, jnp.float32),
        jnp.zeros((count,), jnp.float32),
        jnp.zeros((count, channels), jnp.float32),
    )


def unfold_rows(extended, band_rows, columns):
    pieces_list = [
        extended[row_off : row_off + band_rows, col_off : col_off + columns]
        for row_off in range(3)
        for col_off in range(3)
    ]
    return jnp.concatenate(pieces_list, axis=-1).reshape(band_rows * columns, -1)


def per_device(frames, gain_attn, w_qkv, w_out, gain_conv, w_conv):
    band_rows = frames.shape[1]
    columns = frames.shape[2]
    half_chan = frames.shape[3]
    channels = w_out.shape[0]
    out_half = w_conv.shape[4]
    score_scale = channels ** (-0.5)
    chan_index = lax.axis_index("chan")
    local_bf = frames[0].reshape(-1, half_chan)
    local_x = local_bf.astype(jnp.float32)
    own_gain = lax.dynamic_slice_in_dim(gain_attn, chan_index * half_chan, half_chan)
    scaled = (local_x * own_gain).astype(jnp.bfloat16)
    partial_value = jnp.dot(scaled, w_qkv, preferred_element_type=jnp.float32)
    squares = jnp.sum(local_x * local_x, axis=1)
    placed = lax.dynamic_update_slice_in_dim(
        jnp.zeros((local_x.shape[0], channels), jnp.float32), local_x, chan_index * half_chan, 1
    )
    summed, sum_squares, full_x = (
        lax.psum_scatter(
            partial_value.astype(jnp.bfloat16), "chan", scatter_dimension=0, tiled=True
        ).astype(jnp.float32),
        lax.psum_scatter(
            squares.astype(jnp.bfloat16), "chan", scatter_dimension=0, tiled=True
        ).astype(jnp.float32),
        lax.psum_scatter(
            placed.astype(jnp.bfloat16), "chan", scatter_dimension=0, tiled=True
        ).astype(jnp.float32),
    )
    qkv_rows = (summed * lax.rsqrt(sum_squares[:, None] / channels + epsilon)).astype(jnp.bfloat16)
    queries = qkv_rows[:, :channels]
    key_values = qkv_rows[:, channels:]
    fold_state = online_fold(
        queries,
        channels,
        score_scale,
        empty_state(queries.shape[0], channels),
        lax.all_gather(key_values, ("rows", "chan"), axis=0, tiled=True),
    )
    attended = (fold_state[2] / fold_state[1][:, None]).astype(jnp.bfloat16)
    mixed_rows = (full_x + jnp.dot(attended, w_out, preferred_element_type=jnp.float32)).astype(
        jnp.bfloat16
    )
    band_features = lax.all_gather(
        mixed_rows.reshape(-1, columns, channels), "chan", axis=0, tiled=True
    )
    band_float = band_features.astype(jnp.float32)
    normed = jax.nn.silu(band_float * inv_rms(band_float) * gain_conv).astype(jnp.bfloat16)
    extended = extended_2(normed, (("rows", 0),), 1)
    extended = jnp.pad(extended, ((0, 0), (1, 1), (0, 0)))
    unfolded = unfold_rows(extended, band_rows, columns)
    tap_terms = [
        jnp.dot(
            unfolded, w_conv[tap_index].reshape(-1, out_half), preferred_element_type=jnp.float32
        )
        for tap_index in range(3)
    ]
    result = tap_terms[0]
    for section_index in range(2):
        result = (
            shifted(result.astype(jnp.bfloat16), "tm", 1).astype(result.dtype)
            + tap_terms[section_index + 1]
        )
    return result.astype(jnp.bfloat16).reshape(1, band_rows, columns, out_half)


def solution(mesh):
    in_specs = (
        P(("clips", "tm"), "rows", None, "chan"),
        P(),
        P("chan", None),
        P(),
        P(),
        P(None, None, None, None, "chan"),
    )
    out_specs = P(("clips", "tm"), "rows", None, "chan")
    return jax.shard_map(
        per_device, mesh=mesh, in_specs=in_specs, out_specs=out_specs, check_vma=False
    )
```

profile of v0, /device:TPU:0, one launch (start us, length us, event | category | flops | bytes accessed | tf_op | source)
XLA Modules:
  0.0 107.5 jit_solution(6110074155658979343)
XLA Ops:
  6.5 0.0 all-gather.3.cloned.1.call-start
  6.5 1.1 %copy.15 = f32[1,4,106,192]{2,1,3,0:T(4,128)S(1)} copy(bf16[1,4,106,192]{2,3,1,0:T(8,128)(2,1)} %param.6) | data formatting | bytes 488448 | tf_op jit(solution)/shard_map/convert_element_type | solution.py:75
  7.7 0.0 copy-start.4
  7.7 0.2 reshape.41
  7.9 0.0 copy-start.6
  7.9 0.1 copy.16
  8.1 0.8 dynamic_slice.3
  8.8 2.3 %dynamic_update_slice.3 = bf16[424,384]{1,0:T(8,128)(2,1)S(1)} dynamic-update-slice(bf16[424,384]{1,0:T(8,128)(2,1)S(1)} %broadcast_in_dim.6, bf16[424,192]{1,0:T(8,128)(2,1)S(1)} %copy.16, s32[]{:T(128)} %constant.12.clone.1, s32[]{:T(128)S(6)} %select_n.4) | dynamic-update-slice | bytes 325636 | tf_op jit(solution)/shard_map/dynamic_update_slice | solution.py:80
  11.1 0.6 convolution_convert_fusion
  11.7 4.7 %fusion.39 = (bf16[224,384]{1,0:T(8,128)(2,1)S(1)}, bf16[224,1152]{1,0:T(8,128)(2,1)S(1)}) fusion(bf16[424,384]{1,0:T(8,128)(2,1)S(1)} %dynamic_update_slice.3, bf16[424,1152]{1,0:T(8,128)(2,1)S(1)} %convolution_convert_fusion), kind=kCustom, calls=%all-reduce-scatter.2 | all-reduce-scatter fusion | flops 688129 | bytes 1991168
  16.4 2.3 %collective-permute-start.5 = (bf16[12,1152]{1,0:T(8,128)(2,1)S(1)}, bf16[12,1152]{1,0:T(8,128)(2,1)S(1)}, u32[]{:S(2)}, u32[]{:S(2)}) collective-permute-start(bf16[12,1152]{1,0:T(8,128)(2,1)S(1)} %slice.87), channel_id=1, source_target_pairs={{0,1},{2,3},{4,5},{6,7},{8,9},{10,11},{12,13},{14,15},{16,17},{18,... | collective-permute-start | bytes 82952
  18.7 0.1 multiply_reduce_fusion
  18.8 0.1 convert_element_type.77
  18.9 2.4 %all-reduce.3 = bf16[424]{0:T(512)(128)(2,1)S(1)} all-reduce(bf16[424]{0:T(512)(128)(2,1)S(1)} %convert_element_type.77), channel_id=4, replica_groups=mesh['clips'=2,'tm'=4,'rows'=2,'chan'=2] {'chan'}, use_global_device_ids=true, to_apply=%region_3.0.clone | all-reduce | flops 424 | bytes 1696
  21.3 0.6 fusion.42
  22.6 0.1 add_rsqrt_fusion.1
  23.2 0.0 collective-permute-done.5
  23.2 0.9 concatenate.17
  24.1 0.2 multiply_convert_fusion
  24.3 0.8 slice_bitcast_fusion
  25.1 0.0 all-gather.3.cloned.1.call-update
  25.1 2.2 %collective-permute-start.4 = (bf16[12,384]{1,0:T(8,128)(2,1)S(1)}, bf16[12,384]{1,0:T(8,128)(2,1)S(1)}, u32[]{:S(2)}, u32[]{:S(2)}) collective-permute-start(bf16[12,384]{1,0:T(8,128)(2,1)S(1)} %slice.86), channel_id=1, source_target_pairs={{0,1},{2,3},{4,5},{6,7},{8,9},{10,11},{12,13},{14,15},{16,17},{18,... | collective-permute-start | bytes 27656
  27.3 0.8 collective-permute-done.4
  28.1 0.6 concatenate.16
  28.8 16.8 %all-gather.3.cloned.1.call-done = bf16[4,212,768]{2,1,0:T(8,128)(2,1)} async-done(((bf16[1,212,768]{2,1,0:T(8,128)(2,1)}), bf16[4,212,768]{2,1,0:T(8,128)(2,1)}) %all-gather.3.cloned.1.call-update) | async-done | bytes 1302544 | tf_op jit(solution)/shard_map/all_gather | solution.py:102
  45.6 1.4 %reshape.43 = bf16[848,768]{1,0:T(8,128)(2,1)S(1)} reshape(bf16[4,212,768]{2,1,0:T(8,128)(2,1)} %all-gather.3.cloned.1.call-done) | data formatting | bytes 2605056
  47.0 0.6 fusion.43
  47.6 0.0 copy-start.5
  47.6 0.3 fusion.14
  47.9 0.7 add_convert_fusion.2
  48.7 2.1 %all_gather.7 = bf16[4,106,384]{2,1,0:T(8,128)(2,1)S(1)} all-gather(bf16[2,106,384]{2,1,0:T(8,128)(2,1)S(1)} %reshape.38), channel_id=1, replica_groups=mesh['clips'=2,'tm'=4,'rows'=2,'chan'=2] {'chan'}, dimensions={0}, use_global_device_ids=true | all-gather | bytes 488448 | tf_op jit(solution)/shard_map/all_gather | solution.py:108
  50.7 0.1 fusion.6
  50.9 0.3 fusion.13
  51.2 2.2 %collective-permute-start = (bf16[1,106,384]{2,1,0:T(8,128)(2,1)S(1)}, bf16[1,106,384]{2,1,0:T(8,128)(2,1)S(1)}, u32[]{:S(2)}, u32[]{:S(2)}) collective-permute-start(bf16[1,106,384]{2,1,0:T(8,128)(2,1)S(1)} %get-tuple-element.12), channel_id=1, source_target_pairs={{0,2},{1,3},{4,6},{5,7},{8,10},{9,11},{12,14},{13,15},{16,18},{17,... | collective-permute-start | bytes 244232 | tf_op jit(solution)/shard_map/ppermute | solution.py:14
  53.4 1.3 %collective-permute-start.1 = (bf16[1,106,384]{2,1,0:T(8,128)(2,1)S(1)}, bf16[1,106,384]{2,1,0:T(8,128)(2,1)S(1)}, u32[]{:S(2)}, u32[]{:S(2)}) collective-permute-start(bf16[1,106,384]{2,1,0:T(8,128)(2,1)S(1)} %get-tuple-element.13), channel_id=1, source_target_pairs={{2,0},{3,1},{6,4},{7,5},{10,8},{11,9},{14,12},{15,13},{18,16},{19,... | collective-permute-start | bytes 244232 | tf_op jit(solution)/shard_map/ppermute | solution.py:17
  54.7 4.1 %fusion.40 = (bf16[1,3,3,384,192]{3,4,2,1,0:T(8,128)(2,1)S(1)}, bf16[1,3,3,384,192]{3,4,2,1,0:T(8,128)(2,1)}, bf16[1,3,3,384,192]{3,4,2,1,0:T(8,128)(2,1)}) fusion(bf16[3,3,3,384,192]{3,4,2,1,0:T(8,128)(2,1)} %param.11), kind=kLoop, calls=%fused_computation.57 | loop fusion | bytes 7962624 | tf_op jit(solution)/shard_map/slice | solution.py:118
  58.8 1.1 %copy.17 = bf16[1,3,3,384,192]{3,2,1,4,0:T(4,128)(2,1)S(1)} copy(bf16[1,3,3,384,192]{3,4,2,1,0:T(8,128)(2,1)S(1)} %get-tuple-element.9) | data formatting | bytes 2654208 | tf_op jit(solution)/shard_map/slice | solution.py:118
  60.0 2.3 %reshape_squeeze.10 = bf16[3456,192]{0,1:T(8,128)(2,1)} reshape(bf16[1,3,3,384,192]{3,2,1,4,0:T(4,128)(2,1)S(1)} %copy.17) | data formatting | bytes 2654208 | tf_op jit(solution)/shard_map/reshape;squeeze | solution.py:118
  62.3 0.0 collective-permute-done
  62.3 0.0 collective-permute-done.1
  62.3 0.1 fusion.23
  62.5 0.8 slice_dynamic-update-slice_fusion.5
  63.3 0.8 fusion.29
  64.1 0.9 slice_dynamic-update-slice_fusion.4
  65.0 0.9 slice_dynamic-update-slice_fusion.3
  65.8 1.1 constant_dynamic-update-slice_fusion
  66.9 0.9 slice_dynamic-update-slice_fusion.2
  67.7 0.8 slice_dynamic-update-slice_fusion.1
  68.6 0.8 fusion.28
  69.4 0.8 slice_dynamic-update-slice_fusion
  70.2 2.7 %reshape.39 = bf16[424,3456]{1,0:T(8,128)(2,1)S(1)} reshape(bf16[4,106,3456]{2,1,0:T(8,128)(2,1)} %slice_dynamic-update-slice_fusion) | data formatting | bytes 5861376 | tf_op jit(solution)/shard_map/reshape | solution.py:63
  72.9 4.1 %convolution_convert_fusion.1 = bf16[424,192]{0,1:T(8,128)(2,1)} fusion(bf16[424,3456]{1,0:T(8,128)(2,1)S(1)} %reshape.39, bf16[3456,192]{0,1:T(8,128)(2,1)} %reshape_squeeze.10), kind=kOutput, calls=%fused_computation.6 | convolution fusion | flops 562773504 | bytes 4420608 | tf_op jit(solution)/shard_map/dot_general | solution.py:117
  77.0 4.3 %collective-permute-start.2 = (bf16[424,192]{0,1:T(8,128)(2,1)}, bf16[424,192]{0,1:T(8,128)(2,1)}, u32[]{:S(2)}, u32[]{:S(2)}) collective-permute-start(bf16[424,192]{0,1:T(8,128)(2,1)} %convolution_convert_fusion.1), channel_id=1, source_target_pairs={{0,4},{4,8},{8,12},{1,5},{5,9},{9,13},{2,6},{6,10},{10,14},{3,7},{... | collective-permute-start | bytes 488456 | tf_op jit(solution)/shard_map/ppermute | solution.py:25
  81.3 1.1 %copy.18 = bf16[1,3,3,384,192]{3,2,1,4,0:T(4,128)(2,1)S(1)} copy(bf16[1,3,3,384,192]{3,4,2,1,0:T(8,128)(2,1)S(1)} %copy-done.2) | data formatting | bytes 2654208 | tf_op jit(solution)/shard_map/slice | solution.py:118
  82.5 1.2 %reshape_squeeze.11 = bf16[3456,192]{0,1:T(8,128)(2,1)S(1)} reshape(bf16[1,3,3,384,192]{3,2,1,4,0:T(4,128)(2,1)S(1)} %copy.18) | data formatting | bytes 2654208 | tf_op jit(solution)/shard_map/reshape;squeeze | solution.py:118
  83.7 1.5 %collective-permute-done.2 = bf16[424,192]{0,1:T(8,128)(2,1)} collective-permute-done((bf16[424,192]{0,1:T(8,128)(2,1)}, bf16[424,192]{0,1:T(8,128)(2,1)}, u32[]{:S(2)}, u32[]{:S(2)}) %collective-permute-start.2) | collective-permute-done | bytes 162848 | tf_op jit(solution)/shard_map/ppermute | solution.py:25
  85.2 3.5 %add_convert_fusion.1 = bf16[424,192]{0,1:T(8,128)(2,1)} fusion(bf16[424,192]{0,1:T(8,128)(2,1)} %collective-permute-done.2, bf16[424,3456]{1,0:T(8,128)(2,1)} %copy-done.3, bf16[3456,192]{0,1:T(8,128)(2,1)S(1)} %reshape_squeeze.11), kind=kOutput, calls=%fused_computation.32 | convolution fusion | flops 562936320 | bytes 4583424 | tf_op jit(solution)/shard_map/dot_general | solution.py:117
  88.8 5.1 %collective-permute-start.3 = (bf16[424,192]{0,1:T(8,128)(2,1)}, bf16[424,192]{0,1:T(8,128)(2,1)}, u32[]{:S(2)}, u32[]{:S(2)}) collective-permute-start(bf16[424,192]{0,1:T(8,128)(2,1)} %add_convert_fusion.1), channel_id=1, source_target_pairs={{0,4},{4,8},{8,12},{1,5},{5,9},{9,13},{2,6},{6,10},{10,14},{3,7},{... | collective-permute-start | bytes 488456 | tf_op jit(solution)/shard_map/ppermute | solution.py:25
  93.8 1.1 %copy.19 = bf16[1,3,3,384,192]{3,2,1,4,0:T(4,128)(2,1)S(1)} copy(bf16[1,3,3,384,192]{3,4,2,1,0:T(8,128)(2,1)S(1)} %copy-done.1) | data formatting | bytes 2654208 | tf_op jit(solution)/shard_map/slice | solution.py:118
  95.0 1.2 %reshape_squeeze.12 = bf16[3456,192]{0,1:T(8,128)(2,1)S(1)} reshape(bf16[1,3,3,384,192]{3,2,1,4,0:T(4,128)(2,1)S(1)} %copy.19) | data formatting | bytes 2654208 | tf_op jit(solution)/shard_map/reshape;squeeze | solution.py:118
  96.2 0.7 collective-permute-done.3
  96.9 2.9 %add_convert_fusion = bf16[424,192]{0,1:T(8,128)(2,1)S(1)} fusion(bf16[424,192]{0,1:T(8,128)(2,1)} %collective-permute-done.3, bf16[424,3456]{1,0:T(8,128)(2,1)} %copy-done.3, bf16[3456,192]{0,1:T(8,128)(2,1)S(1)} %reshape_squeeze.12), kind=kOutput, calls=%fused_computation.31 | convolution fusion | flops 562936320 | bytes 4583424 | tf_op jit(solution)/shard_map/dot_general | solution.py:117
  99.7 0.2 reshape.40
  99.9 0.7 copy.20
  (20 shorter events, 0.1 us)
Async XLA Ops:
  6.5 4.6 %copy-start = (bf16[192,1152]{1,0:T(8,128)(2,1)S(1)}, bf16[192,1152]{1,0:T(8,128)(2,1)}, u32[]{:S(2)}) copy-start(bf16[192,1152]{1,0:T(8,128)(2,1)} %param.8) | copy-start | bytes 1327108
  6.5 39.1 %all-gather.3.cloned.1.call-start = ((), (), s32[]{:S(2)}) async-start(), calls=%async_computation | async-start | bytes 1658880 | tf_op jit(solution)/shard_map/all_gather | solution.py:102
  7.7 11.0 %copy-start.4 = (bf16[1,4,106,192]{2,3,1,0:T(8,128)(2,1)S(1)}, bf16[1,4,106,192]{2,3,1,0:T(8,128)(2,1)}, u32[]{:S(2)}) copy-start(bf16[1,4,106,192]{2,3,1,0:T(8,128)(2,1)} %param.6) | copy-start | bytes 488452
  7.9 13.4 %copy-start.6 = (u32[32]{0:T(128)S(1)}, u32[32]{0:T(128)}, u32[]{:S(2)}) copy-start(u32[32]{0:T(128)} %constant.38) | copy-start | bytes 388
  16.4 6.8 %collective-permute-start.5 = (bf16[12,1152]{1,0:T(8,128)(2,1)S(1)}, bf16[12,1152]{1,0:T(8,128)(2,1)S(1)}, u32[]{:S(2)}, u32[]{:S(2)}) collective-permute-start(bf16[12,1152]{1,0:T(8,128)(2,1)S(1)} %slice.87), channel_id=1, source_target_pairs={{0,1},{2,3},{4,5},{6,7},{8,9},{10,11},{12,13},{14,15},{16,17},{18,... | collective-permute-start | bytes 82952
  25.0 22.9 %copy-start.7 = (bf16[384,384]{1,0:T(8,128)(2,1)S(1)}, bf16[384,384]{1,0:T(8,128)(2,1)}, u32[]{:S(2)}) copy-start(bf16[384,384]{1,0:T(8,128)(2,1)} %param.9) | copy-start | bytes 884740
  25.1 3.0 %collective-permute-start.4 = (bf16[12,384]{1,0:T(8,128)(2,1)S(1)}, bf16[12,384]{1,0:T(8,128)(2,1)S(1)}, u32[]{:S(2)}, u32[]{:S(2)}) collective-permute-start(bf16[12,384]{1,0:T(8,128)(2,1)S(1)} %slice.86), channel_id=1, source_target_pairs={{0,1},{2,3},{4,5},{6,7},{8,9},{10,11},{12,13},{14,15},{16,17},{18,... | collective-permute-start | bytes 27656
  47.6 3.3 %copy-start.5 = (f32[384]{0:T(512)S(1)}, f32[384]{0:T(512)}, u32[]{:S(2)}) copy-start(f32[384]{0:T(512)} %param.10) | copy-start | bytes 4612
  51.2 11.1 %collective-permute-start = (bf16[1,106,384]{2,1,0:T(8,128)(2,1)S(1)}, bf16[1,106,384]{2,1,0:T(8,128)(2,1)S(1)}, u32[]{:S(2)}, u32[]{:S(2)}) collective-permute-start(bf16[1,106,384]{2,1,0:T(8,128)(2,1)S(1)} %get-tuple-element.12), channel_id=1, source_target_pairs={{0,2},{1,3},{4,6},{5,7},{8,10},{9,11},{12,14},{13,15},{16,18},{17,... | collective-permute-start | bytes 244232 | tf_op jit(solution)/shard_map/ppermute | solution.py:14
  53.4 8.9 %collective-permute-start.1 = (bf16[1,106,384]{2,1,0:T(8,128)(2,1)S(1)}, bf16[1,106,384]{2,1,0:T(8,128)(2,1)S(1)}, u32[]{:S(2)}, u32[]{:S(2)}) collective-permute-start(bf16[1,106,384]{2,1,0:T(8,128)(2,1)S(1)} %get-tuple-element.13), channel_id=1, source_target_pairs={{2,0},{3,1},{6,4},{7,5},{10,8},{11,9},{14,12},{15,13},{18,16},{19,... | collective-permute-start | bytes 244232 | tf_op jit(solution)/shard_map/ppermute | solution.py:17
  72.9 8.5 %copy-start.3 = (bf16[424,3456]{1,0:T(8,128)(2,1)}, bf16[424,3456]{1,0:T(8,128)(2,1)S(1)}, u32[]{:S(2)}) copy-start(bf16[424,3456]{1,0:T(8,128)(2,1)S(1)} %reshape.39) | copy-start | bytes 8792068
  72.9 8.4 %copy-start.2 = (bf16[1,3,3,384,192]{3,4,2,1,0:T(8,128)(2,1)S(1)}, bf16[1,3,3,384,192]{3,4,2,1,0:T(8,128)(2,1)}, u32[]{:S(2)}) copy-start(bf16[1,3,3,384,192]{3,4,2,1,0:T(8,128)(2,1)} %get-tuple-element.11) | copy-start | bytes 3981316
  77.0 8.2 %collective-permute-start.2 = (bf16[424,192]{0,1:T(8,128)(2,1)}, bf16[424,192]{0,1:T(8,128)(2,1)}, u32[]{:S(2)}, u32[]{:S(2)}) collective-permute-start(bf16[424,192]{0,1:T(8,128)(2,1)} %convolution_convert_fusion.1), channel_id=1, source_target_pairs={{0,4},{4,8},{8,12},{1,5},{5,9},{9,13},{2,6},{6,10},{10,14},{3,7},{... | collective-permute-start | bytes 488456 | tf_op jit(solution)/shard_map/ppermute | solution.py:25
  83.7 10.2 %copy-start.1 = (bf16[1,3,3,384,192]{3,4,2,1,0:T(8,128)(2,1)S(1)}, bf16[1,3,3,384,192]{3,4,2,1,0:T(8,128)(2,1)}, u32[]{:S(2)}) copy-start(bf16[1,3,3,384,192]{3,4,2,1,0:T(8,128)(2,1)} %get-tuple-element.10) | copy-start | bytes 3981316
  88.8 8.1 %collective-permute-start.3 = (bf16[424,192]{0,1:T(8,128)(2,1)}, bf16[424,192]{0,1:T(8,128)(2,1)}, u32[]{:S(2)}, u32[]{:S(2)}) collective-permute-start(bf16[424,192]{0,1:T(8,128)(2,1)} %add_convert_fusion.1), channel_id=1, source_target_pairs={{0,4},{4,8},{8,12},{1,5},{5,9},{9,13},{2,6},{6,10},{10,14},{3,7},{... | collective-permute-start | bytes 488456 | tf_op jit(solution)/shard_map/ppermute | solution.py:25
Sparse Core Ops, SparseCore 0:
  25.2 20.3 all-gather.2
where the time goes:
time: 108 us; the launch traced here: 107 us
  local copies, waits for them, and re-layouts  29.8 us (28%)
  waiting for transfers between devices  19.9 us (18%)
  starting transfers between devices  17.4 us (16%)
  between operations  14.9 us (14%)
  matrix products  12.4 us (11%)
  blocking collectives  9.19 us (9%)
  other arithmetic  3.87 us (4%)
    all_gather x1, waiting for transfers between devices, per_device(): lax.all_gather(key_values, ('rows', 'chan'), axis=0, tiled=True)  16.8 us
    dot_general x3, matrix products, per_device(): jnp.dot(unfolded, w_conv[tap_index].reshape(-1, out_half), preferred_elem...  10.5 us
    ppermute x2, starting transfers between devices, shifted(): return lax.ppermute(array, axis, pairs)  9.37 us
    unnamed x28, local copies, waits for them, and re-layouts  8.54 us
    slice x4, local copies, waits for them, and re-layouts, per_device(): w_conv[tap_index].reshape(-1, out_half)  7.5 us
    unnamed x2, blocking collectives  7.14 us
    another operation x3, local copies, waits for them, and re-layouts, per_device(): w_conv[tap_index].reshape(-1, out_half)  4.72 us
    unnamed x2, starting transfers between devices  4.48 us
  transfers between devices with their start and end apart: 7, of which 4 were waited for; matrix products, arithmetic and copies ran while one was open for 13% of the time, Pallas kernels for 0%

commit v1 on v0

v1 whole, which is shorter than its diff:
```python
import functools

import jax
import jax.numpy as jnp
from jax import lax
from jax.experimental import pallas as pl
from jax.experimental.pallas import tpu as pltpu
from jax.sharding import PartitionSpec as P

epsilon = 1e-06
MESH = pl.DeviceIdType.MESH
f32 = jnp.float32
bf16 = jnp.bfloat16
groups = 2


def padded_columns(columns):
    return -(-columns // 16) * 16


def kernel(
    n_rows, n_tm, x_hbm, ga_ref, wq_hbm, wo_hbm, gc_ref, wc_hbm, out_ref,
    xs, wq, wo, wc, xf, qkv, nb, acc1, acc2, s0, s1, r0, r1,
    local_sem, wsem, xsend, xrecv, zsend, zrecv,
):
    band, columns, half = x_hbm.shape[1:]
    channels = 2 * half
    height = band * n_rows
    wide = xf.shape[1]
    q_rows = band + min(n_rows - 1, 2)
    r = lax.axis_index("rows")
    c = lax.axis_index("chan")
    t = lax.axis_index("tm")
    other = 1 - c

    own_x = pltpu.make_async_copy(x_hbm.at[0], xs.at[r, c], local_sem.at[0])
    own_w = pltpu.make_async_copy(wq_hbm, wq.at[c], local_sem.at[1])
    own_wo = pltpu.make_async_copy(wo_hbm, wo, local_sem.at[2])
    own_wc = pltpu.make_async_copy(wc_hbm, wc, local_sem.at[3])
    own_x.start()
    own_w.start()

    barrier = pltpu.get_barrier_semaphore()
    pl.semaphore_signal(barrier, inc=1, device_id={"chan": other}, device_id_type=MESH)
    for k in range(1, n_rows):
        pl.semaphore_signal(
            barrier, inc=1, device_id={"rows": lax.rem(r + k, n_rows)}, device_id_type=MESH
        )

    @pl.when(t > 0)
    def _():
        pl.semaphore_signal(barrier, inc=1, device_id={"tm": t - 1}, device_id_type=MESH)

    @pl.when(t < n_tm - 1)
    def _():
        pl.semaphore_signal(barrier, inc=1, device_id={"tm": t + 1}, device_id_type=MESH)

    own_wo.start()
    own_wc.start()
    xf[...] = jnp.zeros_like(xf)
    zero_row = jnp.zeros((wide, nb.shape[2]), bf16)
    nb[1] = zero_row
    nb[band + 2] = zero_row
    neighbours = jnp.where(t > 0, 1, 0) + jnp.where(t < n_tm - 1, 1, 0) + n_rows
    pl.semaphore_wait(barrier, neighbours)

    to_rows = []
    for k in range(1, n_rows):
        copy = pltpu.make_async_remote_copy(
            src_ref=x_hbm.at[0], dst_ref=xs.at[r, c], send_sem=xsend.at[k], recv_sem=xrecv.at[r, c],
            device_id={"rows": lax.rem(r + k, n_rows)}, device_id_type=MESH,
        )
        copy.start()
        to_rows.append(copy)
    to_core = pltpu.make_async_remote_copy(
        src_ref=x_hbm.at[0], dst_ref=xs.at[r, c], send_sem=xsend.at[0], recv_sem=xrecv.at[r, c],
        device_id={"chan": other}, device_id_type=MESH,
    )
    to_core.start()
    w_core = pltpu.make_async_remote_copy(
        src_ref=wq_hbm, dst_ref=wq.at[c], send_sem=wsem.at[0], recv_sem=wsem.at[1],
        device_id={"chan": other}, device_id_type=MESH,
    )
    w_core.start()

    def project(who):
        for i in range(band):
            row = jnp.concatenate([xs[who, 0, i].astype(f32), xs[who, 1, i].astype(f32)], axis=-1)
            xf[who * band + i, 0:columns, :] = row.astype(bf16)
        x = xf[pl.ds(who * band, band)].reshape(band * wide, channels).astype(f32)
        inverse = lax.rsqrt(jnp.mean(x * x, axis=-1, keepdims=True) + epsilon)
        u = (x * ga_ref[...]).astype(bf16)
        proj = jnp.dot(u, wq[...].reshape(channels, 3 * channels), preferred_element_type=f32)
        qkv[pl.ds(who * band, band)] = (
            (proj * inverse).astype(bf16).reshape(band, wide, 3 * channels)
        )

    def arrival(slot_r, slot_c, core):
        return pltpu.make_async_remote_copy(
            src_ref=xs.at[slot_r, slot_c], dst_ref=xs.at[slot_r, slot_c],
            send_sem=xsend.at[0], recv_sem=xrecv.at[slot_r, slot_c],
            device_id={"chan": core}, device_id_type=MESH,
        )

    own_x.wait()
    own_w.wait()
    arrival(r, other, other).wait_recv()
    w_core.wait_recv()
    project(r)

    forwards = []
    for k in range(1, n_rows):
        who = lax.rem(r + n_rows - k, n_rows)
        arrival(who, c, other).wait_recv()
        forward = pltpu.make_async_remote_copy(
            src_ref=xs.at[who, c], dst_ref=xs.at[who, c], send_sem=xsend.at[n_rows + k],
            recv_sem=xrecv.at[who, c], device_id={"chan": other}, device_id_type=MESH,
        )
        forward.start()
        forwards.append(forward)
    for k in range(1, n_rows):
        who = lax.rem(r + n_rows - k, n_rows)
        arrival(who, other, other).wait_recv()
        project(who)

    own_wo.wait()
    start = jnp.clip(r * band - 1, 0, height - q_rows)
    count = q_rows * wide
    q = qkv[pl.ds(start, q_rows), :, 0:channels].reshape(count, channels)
    keys = qkv[:, :, channels : 2 * channels].reshape(height * wide, channels)
    values = qkv[:, :, 2 * channels :].reshape(height * wide, channels)
    scores = lax.dot_general(
        q, keys, (((1,), (1,)), ((), ())), preferred_element_type=f32
    ) * (channels ** (-0.5))
    column = lax.broadcasted_iota(jnp.int32, (1, height * wide), 1)
    scores = jnp.where(lax.rem(column, wide) < columns, scores, -jnp.inf)
    exponent = jnp.exp(scores - jnp.max(scores, axis=1, keepdims=True))
    total = jnp.sum(exponent, axis=1, keepdims=True)
    weighted = jnp.dot(exponent.astype(bf16), values, preferred_element_type=f32)
    attended = (weighted / total).astype(bf16)
    x = xf[pl.ds(start, q_rows)].reshape(count, channels).astype(f32)
    mixed = (x + jnp.dot(attended, wo[...], preferred_element_type=f32)).astype(bf16).astype(f32)
    inverse = lax.rsqrt(jnp.mean(mixed * mixed, axis=-1, keepdims=True) + epsilon)
    v = mixed * inverse * gc_ref[...]
    normed = v / (1.0 + jnp.exp(-v))
    token = lax.broadcasted_iota(jnp.int32, (count, 1), 0)
    normed = jnp.where(lax.rem(token, wide) < columns, normed, 0.0)
    place = start - r * band + 2
    for e, shift in enumerate((1, 0, count - 1)):
        moved = pltpu.roll(normed, shift, 0) if shift else normed
        nb[pl.ds(place, q_rows), :, e * channels : (e + 1) * channels] = moved.astype(
            bf16
        ).reshape(q_rows, wide, channels)

    own_wc.wait()
    per = band // groups

    def tap(a, g, n):
        result = None
        for b in range(3):
            lhs = nb[1 + b + g * n : 1 + b + g * n + n].reshape(n * wide, 3 * channels)
            term = jnp.dot(lhs, wc[3 * a + b], preferred_element_type=f32)
            result = term if result is None else result + term
        return result

    def z_copy(stage, g):
        source, target = ((s0, r0), (s1, r1))[stage]
        return pltpu.make_async_remote_copy(
            src_ref=source.at[g], dst_ref=target.at[g], send_sem=zsend.at[stage, g],
            recv_sem=zrecv.at[stage, g], device_id={"tm": jnp.minimum(t + 1, n_tm - 1)},
            device_id_type=MESH,
        )

    for g in range(groups):
        s0[g] = tap(0, g, per).astype(bf16)

        @pl.when(t < n_tm - 1)
        def _():
            z_copy(0, g).start()

    for g in range(groups):
        acc1[g] = tap(1, g, per)

    for g in range(groups):
        @pl.when(t > 0)
        def _():
            z_copy(0, g).wait_recv()
            acc1[g] += r0[g].astype(f32)

        s1[g] = acc1[g].astype(bf16)

        @pl.when(t < n_tm - 1)
        def _():
            z_copy(1, g).start()

    for g in range(groups):
        acc2[g] = tap(2, g, per)

    for g in range(groups):
        @pl.when(t > 0)
        def _():
            z_copy(1, g).wait_recv()
            acc2[g] += r1[g].astype(f32)

        for i in range(per):
            out_ref[0, g * per + i] = acc2[g, i * wide : i * wide + columns, :].astype(bf16)

    for copy in to_rows + forwards + [to_core, w_core]:
        copy.wait_send()

    @pl.when(t < n_tm - 1)
    def _():
        for g in range(groups):
            z_copy(0, g).wait_send()
            z_copy(1, g).wait_send()


def per_device(n_rows, n_tm, frames, gain_attn, w_qkv, w_out, gain_conv, w_conv):
    _, band, columns, half = frames.shape
    channels = w_out.shape[0]
    out_half = w_conv.shape[4]
    height = band * n_rows
    wide = padded_columns(columns)
    per = band // groups
    anywhere = pl.BlockSpec(memory_space=pl.ANY)
    vmem = pl.BlockSpec(memory_space=pltpu.VMEM)
    chunk = (groups, per * wide, out_half)
    return pl.pallas_call(
        functools.partial(kernel, n_rows, n_tm),
        out_shape=jax.ShapeDtypeStruct((1, band, columns, out_half), bf16),
        in_specs=[anywhere, vmem, anywhere, anywhere, vmem, anywhere],
        out_specs=vmem,
        scratch_shapes=[
            pltpu.VMEM((n_rows, 2, band, columns, half), bf16),
            pltpu.VMEM((2, half, 3 * channels), bf16),
            pltpu.VMEM((channels, channels), bf16),
            pltpu.VMEM((9, 3 * channels, out_half), bf16),
            pltpu.VMEM((height, wide, channels), bf16),
            pltpu.VMEM((height, wide, 3 * channels), bf16),
            pltpu.VMEM((band + 4, wide, 3 * channels), bf16),
            pltpu.VMEM(chunk, f32),
            pltpu.VMEM(chunk, f32),
            pltpu.VMEM(chunk, bf16),
            pltpu.VMEM(chunk, bf16),
            pltpu.VMEM(chunk, bf16),
            pltpu.VMEM(chunk, bf16),
            pltpu.SemaphoreType.DMA((4,)),
            pltpu.SemaphoreType.DMA((2,)),
            pltpu.SemaphoreType.DMA((2 * n_rows,)),
            pltpu.SemaphoreType.DMA((n_rows, 2)),
            pltpu.SemaphoreType.DMA((2, groups)),
            pltpu.SemaphoreType.DMA((2, groups)),
        ],
        compiler_params=pltpu.CompilerParams(
            collective_id=0, has_side_effects=True, vmem_limit_bytes=48 * 1024 * 1024
        ),
    )(
        frames, gain_attn.reshape(1, channels), w_qkv, w_out, gain_conv.reshape(1, channels),
        w_conv.reshape(9, 3 * channels, out_half),
    )


def solution(mesh):
    in_specs = (
        P(("clips", "tm"), "rows", None, "chan"),
        P(),
        P("chan", None),
        P(),
        P(),
        P(None, None, None, None, "chan"),
    )
    out_specs = P(("clips", "tm"), "rows", None, "chan")
    return jax.shard_map(
        functools.partial(per_device, mesh.shape["rows"], mesh.shape["tm"]),
        mesh=mesh, in_specs=in_specs, out_specs=out_specs, check_vma=False,
    )
```

time: 108 us -> 37.5 us (0.35)
  the two profiles are of different devices: /device:TPU:0 before, /device:TPU:1 now
where the time goes in v1:
time: 37.5 us; the launch traced here: 37.2 us
  Pallas kernels  25.6 us (68%)
  local copies, waits for them, and re-layouts  11.5 us (31%)
    pallas_call x1, Pallas kernels, per_device(): pl.pallas_call(functools.partial(kernel, n_rows, n_tm), out_shape=jax.Sha...  25.6 us
    unnamed x6, local copies, waits for them, and re-layouts  9.26 us
    pallas_call x1, local copies, waits for them, and re-layouts, per_device(): pl.pallas_call(functools.partial(kernel, n_rows, n_tm), out_shape=jax.Sha...  0.83 us
    reshape x1, local copies, waits for them, and re-layouts, per_device(): gain_attn.reshape(1, channels)  0.75 us

profile of v1, /device:TPU:1, one launch (start us, length us, event | category | flops | bytes accessed | tf_op | source)
XLA Modules:
  0.0 37.2 jit_solution(15725876217171798292)
XLA Ops:
  0.0 0.0 copy-start.1
  0.0 0.0 copy-start
  0.0 0.8 %reshape.9.ga_ref = f32[1,384]{1,0:T(1,128)S(1)} reshape(f32[384]{0:T(512)} %param.7) | data formatting | bytes 3072 | tf_op jit(solution)/shard_map/reshape | solution.py:258
  0.8 0.7 %reshape.10.gc_ref = f32[1,384]{1,0:T(1,128)S(1)} reshape(f32[384]{0:T(512)} %param.10) | data formatting | bytes 3072 | tf_op jit(solution)/shard_map/reshape | solution.py:258
  1.4 1.1 %copy.8.x_hbm = bf16[1,4,106,192]{3,2,1,0:T(8,128)(2,1)S(1)} copy(bf16[1,4,106,192]{2,3,1,0:T(8,128)(2,1)} %param.6) | data formatting | bytes 325632 | tf_op args[0]
  2.5 8.2 %copy.7 = bf16[3,3,3,384,192]{4,3,2,1,0:T(8,128)(2,1)} copy(bf16[3,3,3,384,192]{3,4,2,1,0:T(8,128)(2,1)} %param.11) | data formatting | bytes 7962624 | tf_op args[5]
  10.7 0.0 copy-done.1
  10.7 0.0 copy-done
  10.7 25.6 %shard_map.64 = bf16[1,4,106,192]{3,2,1,0:T(8,128)(2,1)S(1)} custom-call(bf16[1,4,106,192]{3,2,1,0:T(8,128)(2,1)S(1)} %copy.8.x_hbm, f32[1,384]{1,0:T(1,128)S(1)} %reshape.9.ga_ref, bf16[192,1152]{1,0:T(8,128)(2,1)S(1)} %copy-done, bf16[384,384]{1,0:T(8,128)(2,1)S(1)} %copy-done.1, f32[1,384]{1,0:T(1,128)S(1)} %reshape.10.gc_ref, bf16[9,1152,192]{2,1,0:T(8,128)(2,1)} %bitcast.1), custom_call_target="tpu_custom_call" | custom-call | tf_op jit(solution)/shard_map/pallas_call | solution.py:228
  36.3 0.8 %copy.9 = bf16[1,4,106,192]{2,3,1,0:T(8,128)(2,1)} copy(bf16[1,4,106,192]{3,2,1,0:T(8,128)(2,1)S(1)} %shard_map.64) | data formatting | bytes 325632 | tf_op jit(solution)/shard_map/pallas_call | solution.py:228
Async XLA Ops:
  0.0 10.7 %copy-start.1 = (bf16[384,384]{1,0:T(8,128)(2,1)S(1)}, bf16[384,384]{1,0:T(8,128)(2,1)}, u32[]{:S(2)}) copy-start(bf16[384,384]{1,0:T(8,128)(2,1)} %wo_hbm.1) | copy-start | bytes 884740
  0.0 10.7 %copy-start = (bf16[192,1152]{1,0:T(8,128)(2,1)S(1)}, bf16[192,1152]{1,0:T(8,128)(2,1)}, u32[]{:S(2)}) copy-start(bf16[192,1152]{1,0:T(8,128)(2,1)} %wq_hbm.1) | copy-start | bytes 1327108

commit v2 on v1

--- a/solution.py
+++ b/solution.py
@@ -14,19 +14,15 @@
 groups = 2
 
 
-def padded_columns(columns):
-    return -(-columns // 16) * 16
-
-
 def kernel(
     n_rows, n_tm, x_hbm, ga_ref, wq_hbm, wo_hbm, gc_ref, wc_hbm, out_ref,
-    xs, wq, wo, wc, xf, qkv, nb, acc1, acc2, s0, s1, r0, r1,
+    xs, wq, wo, wc, xt, wqt, wot, qt, keys, vt, nb, acc1, acc2, s0, s1, r0, r1,
     local_sem, wsem, xsend, xrecv, zsend, zrecv,
 ):
-    band, columns, half = x_hbm.shape[1:]
+    band, half, columns = x_hbm.shape[1:]
     channels = 2 * half
     height = band * n_rows
-    wide = xf.shape[1]
+    wide = xt.shape[2]
     q_rows = band + min(n_rows - 1, 2)
     r = lax.axis_index("rows")
     c = lax.axis_index("chan")
@@ -57,8 +53,8 @@
 
     own_wo.start()
     own_wc.start()
-    xf[...] = jnp.zeros_like(xf)
-    zero_row = jnp.zeros((wide, nb.shape[2]), bf16)
+    xt[...] = jnp.zeros_like(xt)
+    zero_row = jnp.zeros(nb.shape[1:], bf16)
     nb[1] = zero_row
     nb[band + 2] = zero_row
     neighbours = jnp.where(t > 0, 1, 0) + jnp.where(t < n_tm - 1, 1, 0) + n_rows
@@ -83,17 +79,34 @@
     )
     w_core.start()
 
+    def as_column(gain_ref):
+        return jnp.transpose(jnp.broadcast_to(gain_ref[...], (wide, channels)))
+
+    ga = as_column(ga_ref)
+    gc = as_column(gc_ref)
+
     def project(who):
+        us, inverses = [], []
         for i in range(band):
-            row = jnp.concatenate([xs[who, 0, i].astype(f32), xs[who, 1, i].astype(f32)], axis=-1)
-            xf[who * band + i, 0:columns, :] = row.astype(bf16)
-        x = xf[pl.ds(who * band, band)].reshape(band * wide, channels).astype(f32)
-        inverse = lax.rsqrt(jnp.mean(x * x, axis=-1, keepdims=True) + epsilon)
-        u = (x * ga_ref[...]).astype(bf16)
-        proj = jnp.dot(u, wq[...].reshape(channels, 3 * channels), preferred_element_type=f32)
-        qkv[pl.ds(who * band, band)] = (
-            (proj * inverse).astype(bf16).reshape(band, wide, 3 * channels)
-        )
+            row = who * band + i
+            xt[row, 0:half, 0:columns] = xs[who, 0, i]
+            xt[row, half:channels, 0:columns] = xs[who, 1, i]
+            x = xt[row].astype(f32)
+            us.append((x * ga).astype(bf16))
+            inverses.append(lax.rsqrt(jnp.mean(x * x, axis=0, keepdims=True) + epsilon))
+        u = jnp.concatenate(us, axis=1)
+        inverse = jnp.concatenate(inverses, axis=1)
+
+        def part(index):
+            weights = wqt[index * channels : (index + 1) * channels, :]
+            proj = jnp.dot(weights, u, preferred_element_type=f32)
+            return (proj * inverse).astype(bf16)
+
+        keys[pl.ds(who, 1)] = jnp.transpose(part(1))[None]
+        vt[pl.ds(who, 1)] = part(2)[None]
+        q = part(0)
+        for i in range(band):
+            qt[who * band + i] = q[:, i * wide : (i + 1) * wide]
 
     def arrival(slot_r, slot_c, core):
         return pltpu.make_async_remote_copy(
@@ -102,10 +115,13 @@
             device_id={"chan": core}, device_id_type=MESH,
         )
 
+    own_wo.wait()
+    wot[...] = jnp.transpose(wo[...])
     own_x.wait()
     own_w.wait()
+    w_core.wait_recv()
+    wqt[...] = jnp.transpose(wq[...].reshape(channels, 3 * channels))
     arrival(r, other, other).wait_recv()
-    w_core.wait_recv()
     project(r)
 
     forwards = []
@@ -123,34 +139,33 @@
         arrival(who, other, other).wait_recv()
         project(who)
 
-    own_wo.wait()
     start = jnp.clip(r * band - 1, 0, height - q_rows)
-    count = q_rows * wide
-    q = qkv[pl.ds(start, q_rows), :, 0:channels].reshape(count, channels)
-    keys = qkv[:, :, channels : 2 * channels].reshape(height * wide, channels)
-    values = qkv[:, :, 2 * channels :].reshape(height * wide, channels)
-    scores = lax.dot_general(
-        q, keys, (((1,), (1,)), ((), ())), preferred_element_type=f32
-    ) * (channels ** (-0.5))
-    column = lax.broadcasted_iota(jnp.int32, (1, height * wide), 1)
-    scores = jnp.where(lax.rem(column, wide) < columns, scores, -jnp.inf)
-    exponent = jnp.exp(scores - jnp.max(scores, axis=1, keepdims=True))
-    total = jnp.sum(exponent, axis=1, keepdims=True)
-    weighted = jnp.dot(exponent.astype(bf16), values, preferred_element_type=f32)
-    attended = (weighted / total).astype(bf16)
-    x = xf[pl.ds(start, q_rows)].reshape(count, channels).astype(f32)
-    mixed = (x + jnp.dot(attended, wo[...], preferred_element_type=f32)).astype(bf16).astype(f32)
-    inverse = lax.rsqrt(jnp.mean(mixed * mixed, axis=-1, keepdims=True) + epsilon)
-    v = mixed * inverse * gc_ref[...]
-    normed = v / (1.0 + jnp.exp(-v))
-    token = lax.broadcasted_iota(jnp.int32, (count, 1), 0)
-    normed = jnp.where(lax.rem(token, wide) < columns, normed, 0.0)
     place = start - r * band + 2
-    for e, shift in enumerate((1, 0, count - 1)):
-        moved = pltpu.roll(normed, shift, 0) if shift else normed
-        nb[pl.ds(place, q_rows), :, e * channels : (e + 1) * channels] = moved.astype(
-            bf16
-        ).reshape(q_rows, wide, channels)
+    all_keys = keys[...].reshape(height * wide, channels)
+    all_values = jnp.concatenate([vt[k] for k in range(n_rows)], axis=1)
+    key_cell = lax.rem(lax.broadcasted_iota(jnp.int32, (height * wide, 1), 0), wide)
+    for first in range(0, q_rows, 2):
+        members = range(first, min(first + 2, q_rows))
+        q = jnp.concatenate([qt[start + l] for l in members], axis=1)
+        scores = jnp.dot(all_keys, q, preferred_element_type=f32) * (channels ** (-0.5))
+        scores = jnp.where(key_cell < columns, scores, -jnp.inf)
+        exponent = jnp.exp(scores - jnp.max(scores, axis=0, keepdims=True))
+        total = jnp.sum(exponent, axis=0, keepdims=True)
+        weighted = jnp.dot(all_values, exponent.astype(bf16), preferred_element_type=f32)
+        attended = (weighted / total).astype(bf16)
+        added = jnp.dot(wot[...], attended, preferred_element_type=f32)
+        for l in members:
+            lanes = slice((l - first) * wide, (l - first + 1) * wide)
+            x = xt[start + l].astype(f32)
+            mixed = (x + added[:, lanes]).astype(bf16).astype(f32)
+            inverse = lax.rsqrt(jnp.mean(mixed * mixed, axis=0, keepdims=True) + epsilon)
+            v = mixed * inverse * gc
+            normed = v / (1.0 + jnp.exp(-v))
+            column = lax.broadcasted_iota(jnp.int32, normed.shape, 1)
+            normed = jnp.where(column < columns, normed, 0.0)
+            for e, shift in enumerate((1, 0, wide - 1)):
+                moved = pltpu.roll(normed, shift, 1) if shift else normed
+                nb[place + l, e * channels : (e + 1) * channels, :] = moved.astype(bf16)
 
     own_wc.wait()
     per = band // groups
@@ -158,8 +173,9 @@
     def tap(a, g, n):
         result = None
         for b in range(3):
-            lhs = nb[1 + b + g * n : 1 + b + g * n + n].reshape(n * wide, 3 * channels)
-            term = jnp.dot(lhs, wc[3 * a + b], preferred_element_type=f32)
+            lhs = jnp.concatenate([wc[9 * a + 3 * b + e] for e in range(3)], axis=1)
+            rhs = jnp.concatenate([nb[1 + b + g * n + i] for i in range(n)], axis=1)
+            term = jnp.dot(lhs, rhs, preferred_element_type=f32)
             result = term if result is None else result + term
         return result
 
@@ -203,7 +219,8 @@
             acc2[g] += r1[g].astype(f32)
 
         for i in range(per):
-            out_ref[0, g * per + i] = acc2[g, i * wide : i * wide + columns, :].astype(bf16)
+            done = acc2[g, :, i * wide : (i + 1) * wide].astype(bf16)
+            out_ref[0, g * per + i] = done[:, 0:columns]
 
     for copy in to_rows + forwards + [to_core, w_core]:
         copy.wait_send()
@@ -220,24 +237,27 @@
     channels = w_out.shape[0]
     out_half = w_conv.shape[4]
     height = band * n_rows
-    wide = padded_columns(columns)
-    per = band // groups
+    wide = -(-columns // 128) * 128
     anywhere = pl.BlockSpec(memory_space=pl.ANY)
     vmem = pl.BlockSpec(memory_space=pltpu.VMEM)
-    chunk = (groups, per * wide, out_half)
-    return pl.pallas_call(
+    chunk = (groups, out_half, band // groups * wide)
+    result = pl.pallas_call(
         functools.partial(kernel, n_rows, n_tm),
-        out_shape=jax.ShapeDtypeStruct((1, band, columns, out_half), bf16),
+        out_shape=jax.ShapeDtypeStruct((1, band, out_half, columns), bf16),
         in_specs=[anywhere, vmem, anywhere, anywhere, vmem, anywhere],
         out_specs=vmem,
         scratch_shapes=[
-            pltpu.VMEM((n_rows, 2, band, columns, half), bf16),
+            pltpu.VMEM((n_rows, 2, band, half, columns), bf16),
             pltpu.VMEM((2, half, 3 * channels), bf16),
             pltpu.VMEM((channels, channels), bf16),
-            pltpu.VMEM((9, 3 * channels, out_half), bf16),
-            pltpu.VMEM((height, wide, channels), bf16),
-            pltpu.VMEM((height, wide, 3 * channels), bf16),
-            pltpu.VMEM((band + 4, wide, 3 * channels), bf16),
+            pltpu.VMEM((27, out_half, channels), bf16),
+            pltpu.VMEM((height, channels, wide), bf16),
+            pltpu.VMEM((3 * channels, channels), bf16),
+            pltpu.VMEM((channels, channels), bf16),
+            pltpu.VMEM((height, channels, wide), bf16),
+            pltpu.VMEM((n_rows, band * wide, channels), bf16),
+            pltpu.VMEM((n_rows, channels, band * wide), bf16),
+            pltpu.VMEM((band + 4, 3 * channels, wide), bf16),
             pltpu.VMEM(chunk, f32),
             pltpu.VMEM(chunk, f32),
             pltpu.VMEM(chunk, bf16),
@@ -252,12 +272,14 @@
             pltpu.SemaphoreType.DMA((2, groups)),
         ],
         compiler_params=pltpu.CompilerParams(
-            collective_id=0, has_side_effects=True, vmem_limit_bytes=48 * 1024 * 1024
+            collective_id=0, has_side_effects=True, vmem_limit_bytes=56 * 1024 * 1024
         ),
     )(
-        frames, gain_attn.reshape(1, channels), w_qkv, w_out, gain_conv.reshape(1, channels),
-        w_conv.reshape(9, 3 * channels, out_half),
-    )
+        frames.swapaxes(2, 3), gain_attn.reshape(1, channels), w_qkv, w_out,
+        gain_conv.reshape(1, channels),
+        w_conv.swapaxes(3, 4).reshape(27, out_half, channels),
+    )
+    return result.swapaxes(2, 3)
 
 
 def solution(mesh):

time: 37.5 us -> 29.7 us (0.79)
  the two profiles are of different devices: /device:TPU:1 before, /device:TPU:0 now
where the time goes in v2:
time: 29.7 us; the launch traced here: 29.1 us
  Pallas kernels  25 us (84%)
  local copies, waits for them, and re-layouts  4.12 us (14%)
    pallas_call x1, Pallas kernels, per_device(): pl.pallas_call(functools.partial(kernel, n_rows, n_tm), out_shape=jax.Sha...  25 us
    unnamed x1, local copies, waits for them, and re-layouts  1.62 us
    reshape x1, local copies, waits for them, and re-layouts, per_device(): gain_conv.reshape(1, channels)  1.26 us
    reshape x1, local copies, waits for them, and re-layouts, per_device(): gain_attn.reshape(1, channels)  1.24 us

profile of v2, /device:TPU:0, one launch (start us, length us, event | category | flops | bytes accessed | tf_op | source)
XLA Modules:
  0.0 29.1 jit_solution(8279719481640740270)
XLA Ops:
  0.0 1.2 %reshape.9.ga_ref = f32[1,384]{1,0:T(1,128)} reshape(f32[384]{0:T(512)} %param.7) | data formatting | bytes 3072 | tf_op jit(solution)/shard_map/reshape | solution.py:278
  1.2 1.3 %reshape.10.gc_ref = f32[1,384]{1,0:T(1,128)} reshape(f32[384]{0:T(512)} %param.10) | data formatting | bytes 3072 | tf_op jit(solution)/shard_map/reshape | solution.py:279
  2.5 25.0 %shard_map.64 = bf16[1,4,192,106]{3,2,1,0:T(8,128)(2,1)} custom-call(bf16[1,4,192,106]{3,2,1,0:T(8,128)(2,1)} %bitcast.7, f32[1,384]{1,0:T(1,128)} %reshape.9.ga_ref, bf16[192,1152]{1,0:T(8,128)(2,1)} %wq_hbm.1, bf16[384,384]{1,0:T(8,128)(2,1)} %wo_hbm.1, f32[1,384]{1,0:T(1,128)} %reshape.10.gc_ref, bf16[27,192,384]{2,1,0:T(8,128)(2,1)} %bitcast.5), custom_call_target="tpu_custom_call" | custom-call | tf_op jit(solution)/shard_map/pallas_call | solution.py:244
  27.5 1.6 %copy.8 = bf16[1,4,106,192]{2,3,1,0:T(8,128)(2,1)} copy(bf16[1,4,106,192]{2,3,1,0:T(8,128)(2,1)} %bitcast.6) | data formatting | bytes 325632

commit v3 on v2

v3 whole, which is shorter than its diff:
```python
import functools

import jax
import jax.numpy as jnp
from jax import lax
from jax.experimental import pallas as pl
from jax.experimental.pallas import tpu as pltpu
from jax.sharding import PartitionSpec as P

epsilon = 1e-06
MESH = pl.DeviceIdType.MESH
f32 = jnp.float32
bf16 = jnp.bfloat16
groups = 2


def kernel(
    n_rows, n_tm, x_hbm, ga_ref, wq_hbm, wo_hbm, gc_ref, wc_hbm, out_ref,
    xs, wq, wo, wc, xt, wqt, wot, qt, keys, vt, nb, om, ol, oo, acc1, acc2, s0, s1, r0, r1,
    local_sem, wsem, xsend, xrecv, zsend, zrecv,
):
    band, half, columns = x_hbm.shape[1:]
    channels = 2 * half
    height = band * n_rows
    wide = xt.shape[2]
    start_row = lax.axis_index("rows") * band
    r = lax.axis_index("rows")
    c = lax.axis_index("chan")
    t = lax.axis_index("tm")
    other = 1 - c

    own_x = pltpu.make_async_copy(x_hbm.at[0], xs.at[r, c], local_sem.at[0])
    own_w = pltpu.make_async_copy(wq_hbm, wq.at[c], local_sem.at[1])
    own_wo = pltpu.make_async_copy(wo_hbm, wo, local_sem.at[2])
    own_wc = pltpu.make_async_copy(wc_hbm, wc, local_sem.at[3])
    own_x.start()
    own_w.start()

    barrier = pltpu.get_barrier_semaphore()
    pl.semaphore_signal(barrier, inc=1, device_id={"chan": other}, device_id_type=MESH)
    for k in range(1, n_rows):
        pl.semaphore_signal(
            barrier, inc=1, device_id={"rows": lax.rem(r + k, n_rows)}, device_id_type=MESH
        )

    @pl.when(t > 0)
    def _():
        pl.semaphore_signal(barrier, inc=1, device_id={"tm": t - 1}, device_id_type=MESH)

    @pl.when(t < n_tm - 1)
    def _():
        pl.semaphore_signal(barrier, inc=1, device_id={"tm": t + 1}, device_id_type=MESH)

    own_wo.start()
    own_wc.start()
    xt[...] = jnp.zeros_like(xt)
    zero_row = jnp.zeros(nb.shape[1:], bf16)
    nb[0] = zero_row
    nb[band + 1] = zero_row
    neighbours = jnp.where(t > 0, 1, 0) + jnp.where(t < n_tm - 1, 1, 0) + n_rows
    pl.semaphore_wait(barrier, neighbours)

    sent = []
    for i in range(band):
        for k in range(1, n_rows):
            copy = pltpu.make_async_remote_copy(
                src_ref=x_hbm.at[0, i], dst_ref=xs.at[r, c, i], send_sem=xsend.at[k, i],
                recv_sem=xrecv.at[r, c, i], device_id={"rows": lax.rem(r + k, n_rows)},
                device_id_type=MESH,
            )
            copy.start()
            sent.append(copy)
    w_core = pltpu.make_async_remote_copy(
        src_ref=wq_hbm, dst_ref=wq.at[c], send_sem=wsem.at[0], recv_sem=wsem.at[1],
        device_id={"chan": other}, device_id_type=MESH,
    )
    w_core.start()
    for i in range(band):
        copy = pltpu.make_async_remote_copy(
            src_ref=x_hbm.at[0, i], dst_ref=xs.at[r, c, i], send_sem=xsend.at[0, i],
            recv_sem=xrecv.at[r, c, i], device_id={"chan": other}, device_id_type=MESH,
        )
        copy.start()
        sent.append(copy)

    def as_column(gain_ref):
        return jnp.transpose(jnp.broadcast_to(gain_ref[...][None, :], (wide, channels)))

    ga = as_column(ga_ref)
    gc = as_column(gc_ref)

    def project(who, rows):
        us, inverses = [], []
        for i in rows:
            row = who * band + i
            xt[row, 0:half, 0:columns] = xs[who, 0, i]
            xt[row, half:channels, 0:columns] = xs[who, 1, i]
            x = xt[row].astype(f32)
            us.append((x * ga).astype(bf16))
            inverses.append(lax.rsqrt(jnp.mean(x * x, axis=0, keepdims=True) + epsilon))
        u = jnp.concatenate(us, axis=1)
        inverse = jnp.concatenate(inverses, axis=1)
        lanes = slice(rows[0] * wide, (rows[-1] + 1) * wide)

        def part(index):
            weights = wqt[index * channels : (index + 1) * channels, :]
            proj = jnp.dot(weights, u, preferred_element_type=f32)
            return (proj * inverse).astype(bf16)

        keys[pl.ds(who, 1), lanes, :] = jnp.transpose(part(1))[None]
        vt[pl.ds(who, 1), :, lanes] = part(2)[None]
        q = part(0)
        for n, i in enumerate(rows):
            qt[who * band + i] = q[:, n * wide : (n + 1) * wide]

    key_cell = lax.rem(lax.broadcasted_iota(jnp.int32, (band * wide, 1), 0), wide)

    def fold(q, who, state):
        scores = jnp.dot(keys[who], q, preferred_element_type=f32) * (channels ** (-0.5))
        scores = jnp.where(key_cell < columns, scores, -jnp.inf)
        largest = jnp.max(scores, axis=0, keepdims=True)
        if state is not None:
            largest = jnp.maximum(largest, state[0])
        exponent = jnp.exp(scores - largest)
        total = jnp.sum(exponent, axis=0, keepdims=True)
        weighted = jnp.dot(vt[who], exponent.astype(bf16), preferred_element_type=f32)
        if state is not None:
            factor = jnp.exp(state[0] - largest)
            total = total + state[1] * factor
            weighted = weighted + state[2] * factor
        return largest, total, weighted

    def finish(state, members):
        attended = (state[2] / state[1]).astype(bf16)
        added = jnp.dot(wot[...], attended, preferred_element_type=f32)
        for n, (row, slot, valid) in enumerate(members):
            x = xt[row].astype(f32)
            mixed = (x + added[:, n * wide : (n + 1) * wide]).astype(bf16).astype(f32)
            inverse = lax.rsqrt(jnp.mean(mixed * mixed, axis=0, keepdims=True) + epsilon)
            v = mixed * inverse * gc
            normed = v / (1.0 + jnp.exp(-v))
            column = lax.broadcasted_iota(jnp.int32, normed.shape, 1)
            inside = column < (columns if valid is None else jnp.where(valid, columns, 0))
            normed = jnp.where(inside, normed, 0.0)
            for e, shift in enumerate((1, 0, wide - 1)):
                moved = pltpu.roll(normed, shift, 1) if shift else normed
                nb[slot, e * channels : (e + 1) * channels, :] = moved.astype(bf16)

    def arrive(slot_r, slot_c, i):
        pltpu.make_async_remote_copy(
            src_ref=xs.at[slot_r, slot_c, i], dst_ref=xs.at[slot_r, slot_c, i],
            send_sem=xsend.at[0, i], recv_sem=xrecv.at[slot_r, slot_c, i],
            device_id={"chan": other}, device_id_type=MESH,
        ).wait_recv()

    own_wo.wait()
    wot[...] = jnp.transpose(wo[...])
    own_x.wait()
    own_w.wait()
    w_core.wait_recv()
    wqt[...] = jnp.transpose(wq[...].reshape(channels, 3 * channels))
    for i in range(band):
        arrive(r, other, i)
    project(r, range(band))

    per = band // groups

    def own_queries(g):
        return jnp.concatenate([qt[start_row + g * per + i] for i in range(per)], axis=1)

    def keep(g, state):
        om[g], ol[g], oo[g] = state

    def own_fold(g):
        keep(g, fold(own_queries(g), r, None))

    def pass_on(k, rows):
        who = lax.rem(r + n_rows - k, n_rows)
        for i in rows:
            arrive(who, c, i)
            copy = pltpu.make_async_remote_copy(
                src_ref=xs.at[who, c, i], dst_ref=xs.at[who, c, i],
                send_sem=xsend.at[n_rows + k - 1, i], recv_sem=xrecv.at[who, c, i],
                device_id={"chan": other}, device_id_type=MESH,
            )
            copy.start()
            sent.append(copy)

    for g in range(groups):
        own_fold(g)
        for k in range(1, n_rows):
            pass_on(k, range(g * per, (g + 1) * per))
    for k in range(1, n_rows):
        who = lax.rem(r + n_rows - k, n_rows)
        for g in range(2):
            rows = range(g * band // 2, (g + 1) * band // 2)
            for i in rows:
                arrive(who, other, i)
            project(who, rows)

    def rest(g):
        state = om[g], ol[g], oo[g]
        q = own_queries(g)
        for k in range(1, n_rows):
            state = fold(q, lax.rem(r + n_rows - k, n_rows), state)
        members = [
            (start_row + g * per + i, 1 + g * per + i, None) for i in range(per)
        ]
        finish(state, members)

    if n_rows == 2:
        below = r > 0
        halo = [
            (jnp.where(below, start_row - 1, start_row + band), jnp.where(below, 0, band + 1), None)
        ]
    elif n_rows > 2:
        halo = [
            (jnp.maximum(start_row - 1, 0), 0, r > 0),
            (jnp.minimum(start_row + band, height - 1), band + 1, r < n_rows - 1),
        ]
    else:
        halo = []

    def halo_rows():
        if halo:
            q = jnp.concatenate([qt[row] for row, _, _ in halo], axis=1)
            state = None
            for k in range(n_rows):
                state = fold(q, lax.rem(r + n_rows - k, n_rows), state)
            finish(state, halo)

    def tap(a, g):
        result = None
        for b in range(3):
            lhs = jnp.concatenate([wc[9 * a + 3 * b + e] for e in range(3)], axis=1)
            rhs = jnp.concatenate([nb[b + g * per + i] for i in range(per)], axis=1)
            term = jnp.dot(lhs, rhs, preferred_element_type=f32)
            result = term if result is None else result + term
        return result

    def z_copy(stage, g):
        source, target = ((s0, r0), (s1, r1))[stage]
        return pltpu.make_async_remote_copy(
            src_ref=source.at[g], dst_ref=target.at[g], send_sem=zsend.at[stage, g],
            recv_sem=zrecv.at[stage, g], device_id={"tm": jnp.minimum(t + 1, n_tm - 1)},
            device_id_type=MESH,
        )

    def first_tap(g):
        s0[g] = tap(0, g).astype(bf16)

        @pl.when(t < n_tm - 1)
        def _():
            z_copy(0, g).start()

    lead = r if n_rows == 2 else 0
    order = (lead, 1 - lead)
    for g in range(groups):
        rest(g)
    if n_rows > 2:
        halo_rows()
    own_wc.wait()
    first_tap(order[0])
    if n_rows <= 2:
        halo_rows()
    first_tap(order[1])

    for g in order:
        acc1[g] = tap(1, g)

    for g in order:
        @pl.when(t > 0)
        def _():
            z_copy(0, g).wait_recv()
            acc1[g] += r0[g].astype(f32)

        s1[g] = acc1[g].astype(bf16)

        @pl.when(t < n_tm - 1)
        def _():
            z_copy(1, g).start()

    for g in order:
        acc2[g] = tap(2, g)

    for g in order:
        @pl.when(t > 0)
        def _():
            z_copy(1, g).wait_recv()
            acc2[g] += r1[g].astype(f32)

        for i in range(per):
            done = acc2[g, :, i * wide : (i + 1) * wide].astype(bf16)
            out_ref[0, g * per + i] = done[:, 0:columns]

    for copy in sent + [w_core]:
        copy.wait_send()

    @pl.when(t < n_tm - 1)
    def _():
        for g in range(groups):
            z_copy(0, g).wait_send()
            z_copy(1, g).wait_send()


def per_device(n_rows, n_tm, frames, gain_attn, w_qkv, w_out, gain_conv, w_conv):
    _, band, columns, half = frames.shape
    channels = w_out.shape[0]
    out_half = w_conv.shape[4]
    height = band * n_rows
    wide = -(-columns // 128) * 128
    anywhere = pl.BlockSpec(memory_space=pl.ANY)
    vmem = pl.BlockSpec(memory_space=pltpu.VMEM)
    chunk = (groups, out_half, band // groups * wide)
    result = pl.pallas_call(
        functools.partial(kernel, n_rows, n_tm),
        out_shape=jax.ShapeDtypeStruct((1, band, out_half, columns), bf16),
        in_specs=[anywhere, vmem, anywhere, anywhere, vmem, anywhere],
        out_specs=vmem,
        scratch_shapes=[
            pltpu.VMEM((n_rows, 2, band, half, columns), bf16),
            pltpu.VMEM((2, half, 3 * channels), bf16),
            pltpu.VMEM((channels, channels), bf16),
            pltpu.VMEM((27, out_half, channels), bf16),
            pltpu.VMEM((height, channels, wide), bf16),
            pltpu.VMEM((3 * channels, channels), bf16),
            pltpu.VMEM((channels, channels), bf16),
            pltpu.VMEM((height, channels, wide), bf16),
            pltpu.VMEM((n_rows, band * wide, channels), bf16),
            pltpu.VMEM((n_rows, channels, band * wide), bf16),
            pltpu.VMEM((band + 2, 3 * channels, wide), bf16),
            pltpu.VMEM((groups, 1, band // groups * wide), f32),
            pltpu.VMEM((groups, 1, band // groups * wide), f32),
            pltpu.VMEM((groups, channels, band // groups * wide), f32),
            pltpu.VMEM(chunk, f32),
            pltpu.VMEM(chunk, f32),
            pltpu.VMEM(chunk, bf16),
            pltpu.VMEM(chunk, bf16),
            pltpu.VMEM(chunk, bf16),
            pltpu.VMEM(chunk, bf16),
            pltpu.SemaphoreType.DMA((4,)),
            pltpu.SemaphoreType.DMA((2,)),
            pltpu.SemaphoreType.DMA((2 * n_rows, band)),
            pltpu.SemaphoreType.DMA((n_rows, 2, band)),
            pltpu.SemaphoreType.DMA((2, groups)),
            pltpu.SemaphoreType.DMA((2, groups)),
        ],
        compiler_params=pltpu.CompilerParams(
            collective_id=0, has_side_effects=True, vmem_limit_bytes=56 * 1024 * 1024
        ),
    )(
        frames.swapaxes(2, 3), gain_attn, w_qkv, w_out,
        gain_conv,
        w_conv.swapaxes(3, 4).reshape(27, out_half, channels),
    )
    return result.swapaxes(2, 3)


def solution(mesh):
    in_specs = (
        P(("clips", "tm"), "rows", None, "chan"),
        P(),
        P("chan", None),
        P(),
        P(),
        P(None, None, None, None, "chan"),
    )
    out_specs = P(("clips", "tm"), "rows", None, "chan")
    return jax.shard_map(
        functools.partial(per_device, mesh.shape["rows"], mesh.shape["tm"]),
        mesh=mesh, in_specs=in_specs, out_specs=out_specs, check_vma=False,
    )
```

time: 29.7 us -> 26.7 us (0.90); the launches traced: 29.1 us -> 26.6 us
  local copies, waits for them, and re-layouts: 4.12 us -> 1.62 us
    reshape x2 -> x0, local copies, waits for them, and re-layouts: 2.5 us -> none  [the longest x1 1.26 us: per_device(): gain_conv.reshape(1, channels)]
where the time goes in v3:
time: 26.7 us; the launch traced here: 26.6 us
  Pallas kernels  24.9 us (93%)
  local copies, waits for them, and re-layouts  1.62 us (6%)
    pallas_call x1, Pallas kernels, per_device(): pl.pallas_call(functools.partial(kernel, n_rows, n_tm), out_shape=jax.Sha...  24.9 us
    unnamed x1, local copies, waits for them, and re-layouts  1.62 us

profile of v3, /device:TPU:0, one launch (start us, length us, event | category | flops | bytes accessed | tf_op | source)
XLA Modules:
  0.0 26.6 jit_solution(16254223093370859651)
XLA Ops:
  0.0 24.9 %shard_map.64 = bf16[1,4,192,106]{3,2,1,0:T(8,128)(2,1)} custom-call(bf16[1,4,192,106]{3,2,1,0:T(8,128)(2,1)} %bitcast.7, f32[384]{0:T(512)} %ga_ref.1, bf16[192,1152]{1,0:T(8,128)(2,1)} %wq_hbm.1, bf16[384,384]{1,0:T(8,128)(2,1)} %wo_hbm.1, f32[384]{0:T(512)} %gc_ref.1, bf16[27,192,384]{2,1,0:T(8,128)(2,1)} %bitcast.5), custom_call_target="tpu_custom_call" | custom-call | tf_op jit(solution)/shard_map/pallas_call | solution.py:315
  24.9 1.6 %copy.8 = bf16[1,4,106,192]{2,3,1,0:T(8,128)(2,1)} copy(bf16[1,4,106,192]{2,3,1,0:T(8,128)(2,1)} %bitcast.6) | data formatting | bytes 325632

commit v4 on v3

--- a/solution.py
+++ b/solution.py
@@ -12,6 +12,51 @@
 f32 = jnp.float32
 bf16 = jnp.bfloat16
 groups = 2
+
+
+def packs(out_half, columns, wide, per):
+    left = per * columns - wide
+    return per == 2 and 64 < left < 128 and wide == 128 and out_half % (16 * (wide // (left - 64))) == 0
+
+
+def pack(value, columns):
+    out_half, wide = value.shape[0], value.shape[1] // 2
+    taken = wide - columns
+    narrow = columns - taken - 64
+    pieces = wide // narrow
+    step = out_half // pieces
+    second = value[:, wide:]
+    full = jnp.concatenate([value[:, 0:columns], second[:, 0:taken]], axis=1)
+    middle = second[:, taken : taken + 64]
+    middle = jnp.concatenate([middle[: out_half // 2], middle[out_half // 2 :]], axis=1)
+    last = second[:, taken + 64 : columns]
+    last = [last[p * step : (p + 1) * step] for p in range(pieces)]
+    last.append(jnp.zeros((step, wide - pieces * narrow), f32))
+    return jnp.concatenate([full, middle, jnp.concatenate(last, axis=1)], axis=0).astype(bf16)
+
+
+def unpack(ref_value, out_half, columns):
+    value = ref_value.astype(f32)
+    wide = value.shape[1]
+    taken = wide - columns
+    narrow = columns - taken - 64
+    pieces = wide // narrow
+    full = value[0:out_half]
+    middle = value[out_half : out_half + out_half // 2]
+    last = value[out_half + out_half // 2 :]
+    pad = jnp.zeros((out_half, taken), f32)
+    second = jnp.concatenate(
+        [
+            full[:, columns:],
+            jnp.concatenate([middle[:, 0:64], middle[:, 64:128]], axis=0),
+            jnp.concatenate(
+                [last[:, p * narrow : (p + 1) * narrow] for p in range(pieces)], axis=0
+            ),
+            pad,
+        ],
+        axis=1,
+    )
+    return jnp.concatenate([full[:, 0:columns], pad, second], axis=1)
 
 
 def kernel(
@@ -246,8 +291,16 @@
             device_id_type=MESH,
         )
 
+    packed = packs(half, columns, wide, per)
+
+    def pressed(value):
+        return pack(value, columns) if packed else value.astype(bf16)
+
+    def spread(value):
+        return unpack(value, half, columns) if packed else value.astype(f32)
+
     def first_tap(g):
-        s0[g] = tap(0, g).astype(bf16)
+        s0[g] = pressed(tap(0, g))
 
         @pl.when(t < n_tm - 1)
         def _():
@@ -272,9 +325,9 @@
         @pl.when(t > 0)
         def _():
             z_copy(0, g).wait_recv()
-            acc1[g] += r0[g].astype(f32)
-
-        s1[g] = acc1[g].astype(bf16)
+            acc1[g] += spread(r0[g])
+
+        s1[g] = pressed(acc1[g])
 
         @pl.when(t < n_tm - 1)
         def _():
@@ -287,7 +340,7 @@
         @pl.when(t > 0)
         def _():
             z_copy(1, g).wait_recv()
-            acc2[g] += r1[g].astype(f32)
+            acc2[g] += spread(r1[g])
 
         for i in range(per):
             done = acc2[g, :, i * wide : (i + 1) * wide].astype(bf16)
@@ -312,6 +365,10 @@
     anywhere = pl.BlockSpec(memory_space=pl.ANY)
     vmem = pl.BlockSpec(memory_space=pltpu.VMEM)
     chunk = (groups, out_half, band // groups * wide)
+    travel = chunk
+    if packs(out_half, columns, wide, band // groups):
+        left = (band // groups) * columns - wide - 64
+        travel = (groups, out_half + out_half // 2 + out_half // (wide // left), wide)
     result = pl.pallas_call(
         functools.partial(kernel, n_rows, n_tm),
         out_shape=jax.ShapeDtypeStruct((1, band, out_half, columns), bf16),
@@ -334,10 +391,10 @@
             pltpu.VMEM((groups, channels, band // groups * wide), f32),
             pltpu.VMEM(chunk, f32),
             pltpu.VMEM(chunk, f32),
-            pltpu.VMEM(chunk, bf16),
-            pltpu.VMEM(chunk, bf16),
-            pltpu.VMEM(chunk, bf16),
-            pltpu.VMEM(chunk, bf16),
+            pltpu.VMEM(travel, bf16),
+            pltpu.VMEM(travel, bf16),
+            pltpu.VMEM(travel, bf16),
+            pltpu.VMEM(travel, bf16),
             pltpu.SemaphoreType.DMA((4,)),
             pltpu.SemaphoreType.DMA((2,)),
             pltpu.SemaphoreType.DMA((2 * n_rows, band)),

time: 26.7 us -> 25.8 us (0.966)
  Pallas kernels: 24.9 us -> 24 us
    pallas_call x1, Pallas kernels: 24.9 us -> 24 us  [per_device(): pl.pallas_call(functools.partial(kernel, n_rows, n_tm), out_shape=jax.Sha...]
where the time goes in v4:
time: 25.8 us; the launch traced here: 25.7 us
  Pallas kernels  24 us (93%)
  local copies, waits for them, and re-layouts  1.62 us (6%)
    pallas_call x1, Pallas kernels, per_device(): pl.pallas_call(functools.partial(kernel, n_rows, n_tm), out_shape=jax.Sha...  24 us
    unnamed x1, local copies, waits for them, and re-layouts  1.62 us

profile of v4, /device:TPU:0, one launch (start us, length us, event | category | flops | bytes accessed | tf_op | source)
XLA Modules:
  0.0 25.7 jit_solution(15822558912282942800)
XLA Ops:
  0.0 24.0 %shard_map.64 = bf16[1,4,192,106]{3,2,1,0:T(8,128)(2,1)} custom-call(bf16[1,4,192,106]{3,2,1,0:T(8,128)(2,1)} %bitcast.7, f32[384]{0:T(512)} %ga_ref.1, bf16[192,1152]{1,0:T(8,128)(2,1)} %wq_hbm.1, bf16[384,384]{1,0:T(8,128)(2,1)} %wo_hbm.1, f32[384]{0:T(512)} %gc_ref.1, bf16[27,192,384]{2,1,0:T(8,128)(2,1)} %bitcast.5), custom_call_target="tpu_custom_call" | custom-call | tf_op jit(solution)/shard_map/pallas_call | solution.py:372
  24.1 1.6 %copy.8 = bf16[1,4,106,192]{2,3,1,0:T(8,128)(2,1)} copy(bf16[1,4,106,192]{2,3,1,0:T(8,128)(2,1)} %bitcast.6) | data formatting | bytes 325632
